TPU v7x, 32 devices: a whole 2x2x4 slice. The times are simulated.
32 devices in a mesh: grp: 2 (over y), seq: 4 (over z), head: 2 (over x), sub: 2 (over core).
Axes of the slice: x: 2, y: 2, z: 4, core: 2. Of those that a mesh axis runs over, the one named last changes fastest.
Arguments:
- vid_q: bfloat16 [2560, 4096], P(('grp', 'seq', 'sub'), 'head'), parts along dimension 0, may hold values from -6 to 6
- vid_k: bfloat16 [2560, 4096], P(('grp', 'seq', 'sub'), 'head'), parts along dimension 0, may hold values from -6 to 6
- vid_v: bfloat16 [2560, 4096], P(('grp', 'seq', 'sub'), 'head'), parts along dimension 0, may hold values from -6 to 6
- aud_q: bfloat16 [640, 2048], P(('grp', 'seq', 'sub'), 'head'), parts along dimension 0, may hold values from -6 to 6
- cross_k: bfloat16 [2560, 2048], P(('grp', 'seq', 'sub'), 'head'), parts along dimension 0, may hold values from -6 to 6
- cross_v: bfloat16 [2560, 2048], P(('grp', 'seq', 'sub'), 'head'), parts along dimension 0, may hold values from -6 to 6
- cross_q: bfloat16 [2560, 2048], P(('grp', 'seq', 'sub'), 'head'), parts along dimension 0, may hold values from -6 to 6
- aud_k: bfloat16 [640, 2048], P(('grp', 'seq', 'sub'), 'head'), parts along dimension 0, may hold values from -6 to 6
- aud_v: bfloat16 [640, 2048], P(('grp', 'seq', 'sub'), 'head'), parts along dimension 0, may hold values from -6 to 6
- windows: int32 [2, 80], P(None, 'grp'), parts along dimension 1, may hold values from 0 to 40, as said below
Outputs:
- video_self: bfloat16 [2560, 4096], P(('grp', 'seq', 'sub'), 'head'), parts along dimension 0
- audio_out: bfloat16 [640, 2048], P(('grp', 'seq', 'sub'), 'head'), parts along dimension 0
- video_cross: bfloat16 [2560, 2048], P(('grp', 'seq', 'sub'), 'head'), parts along dimension 0
There are 2 independent parts, one for each index of `grp`. A program takes and returns all parts, laid end to end along the dimension named above; each array names one. Nothing has to cross between parts.
Inputs may be any that keep to these rules, and one draw needn't show every extreme that they name: For every stretch c, windows[0, c] lies between max(0, c - 5) and c, and windows[1, c] between c + 1 and min(40, c + 6); in every draw some stretch reaches 5 tiles on both sides.
All inputs are finite; a program needn't handle non-finite values.
Results may differ from a plain program's by a relative error of at most 0.03.
Values may be sent and summed in bfloat16 or wider, within the bound.
A program may use at most 64 MiB of HBM per device.

v0:
```python
from functools import partial
import math
import jax
import jax.numpy as jnp
from jax import lax
from jax.sharding import PartitionSpec as P

HEAD_DIM = 128
AUDIO_DIM = 64
TILE_LEN = 32
STRETCH_LEN = 8


def extended(cells, sides, width):
    for axis, dim in sides:
        count = lax.axis_size(axis)
        ends = count - 1
        head = lax.slice_in_dim(cells, 0, width, axis=dim)
        tail = lax.slice_in_dim(cells, cells.shape[dim] - width, cells.shape[dim], axis=dim)
        cells = jnp.concatenate(
            [
                lax.ppermute(tail, axis, [(i, (i + 1) % count) for i in range(ends)]),
                cells,
                lax.ppermute(head, axis, [((i + 1) % count, i) for i in range(ends)]),
            ],
            axis=dim,
        )
    return cells


def start_state(query_count, head_count, head_size):
    running = jnp.full((head_count, query_count), -jnp.inf, jnp.float32)
    summed = jnp.zeros((head_count, query_count), jnp.float32)
    numerator = jnp.zeros((head_count, query_count, head_size), jnp.float32)
    return (running, summed, numerator)


def absorb(state_in, queries, key_rows, value_rows, head_count, scaling, visible):
    running, summed, numerator = state_in
    query_count = queries.shape[0]
    key_count = key_rows.shape[0]
    head_size = queries.shape[1] // head_count
    scores = (
        jnp.einsum(
            "qhe,khe->hqk",
            queries.reshape(query_count, head_count, head_size),
            key_rows.reshape(key_count, head_count, head_size),
            preferred_element_type=jnp.float32,
        )
        * scaling
    )
    if visible is not None:
        scores = jnp.where(visible[None], scores, jnp.float32(-1e30))
    newest = jnp.maximum(running, jnp.max(scores, axis=2))
    shrink = jnp.exp(running - newest)
    weights = jnp.exp(scores - newest[:, :, None])
    summed = summed * shrink + jnp.sum(weights, axis=2)
    numerator = numerator * shrink[:, :, None] + jnp.einsum(
        "hqk,khe->hqe",
        weights.astype(jnp.bfloat16),
        value_rows.reshape(key_count, head_count, head_size),
        preferred_element_type=jnp.float32,
    )
    return (newest, summed, numerator)


def block_split(total_rows):
    block_rows = total_rows
    while block_rows > 512 and block_rows % 2 == 0:
        block_rows = block_rows // 2
    return (block_rows, total_rows // block_rows)


def fold_keys(state_in, shards_in, offset, queries, head_count, scaling):
    key_rows, value_rows = shards_in
    block_rows, block_count = block_split(key_rows.shape[0])
    key_blocks = key_rows.reshape(block_count, block_rows, key_rows.shape[1])
    value_blocks = value_rows.reshape(block_count, block_rows, value_rows.shape[1])

    def one_block(state, paired):
        return (absorb(state, queries, paired[0], paired[1], head_count, scaling, None), None)

    result, unused = lax.scan(one_block, state_in, (key_blocks, value_blocks))
    return result


def normalize_heads(state_in):
    running, summed, numerator = state_in
    mixed = numerator / summed[:, :, None]
    return mixed.transpose(1, 0, 2).reshape(mixed.shape[1], -1).astype(jnp.bfloat16)


def body(vid_q, vid_k, vid_v, aud_q, cross_k, cross_v, cross_q, aud_k, aud_v, windows):
    video_heads = vid_q.shape[1] // HEAD_DIM
    video_scaling = 1.0 / math.sqrt(HEAD_DIM)
    audio_heads = aud_q.shape[1] // AUDIO_DIM
    audio_scaling = 1.0 / math.sqrt(AUDIO_DIM)
    moved_q, moved_k, moved_v = (
        lax.all_to_all(vid_q, "sub", split_axis=1, concat_axis=0, tiled=True),
        lax.all_to_all(vid_k, "sub", split_axis=1, concat_axis=0, tiled=True),
        lax.all_to_all(vid_v, "sub", split_axis=1, concat_axis=0, tiled=True),
    )
    pair_heads = video_heads // lax.axis_size("sub")
    folder = partial(fold_keys, queries=moved_q, head_count=pair_heads, scaling=video_scaling)
    state = folder(
        start_state(moved_q.shape[0], pair_heads, HEAD_DIM),
        (
            lax.all_gather(moved_k, "seq", axis=0, tiled=True),
            lax.all_gather(moved_v, "seq", axis=0, tiled=True),
        ),
        jnp.int32(0),
    )
    video_self = lax.all_to_all(
        normalize_heads(state), "sub", split_axis=0, concat_axis=1, tiled=True
    )
    folder = partial(fold_keys, queries=aud_q, head_count=audio_heads, scaling=audio_scaling)
    state = folder(
        start_state(aud_q.shape[0], audio_heads, AUDIO_DIM),
        (
            lax.all_gather(cross_k, ("seq", "sub"), axis=0, tiled=True),
            lax.all_gather(cross_v, ("seq", "sub"), axis=0, tiled=True),
        ),
        jnp.int32(0),
    )
    audio_out = normalize_heads(state)
    audio_rows = aud_k.shape[0]
    key_width = aud_k.shape[1]
    padded_rows = extended(
        jnp.concatenate((aud_k, aud_v), axis=1), ((("seq", "sub"), 0),), audio_rows
    )
    near_keys = padded_rows[:, :key_width]
    near_values = padded_rows[:, key_width:]
    position = lax.axis_index(("seq", "sub"))
    audio_index = (position - 1) * audio_rows + jnp.arange(padded_rows.shape[0], dtype=jnp.int32)
    stretch_index = audio_index // STRETCH_LEN
    stretch_ids = jnp.arange(windows.shape[1], dtype=jnp.int32)
    onehot = stretch_index[:, None] == stretch_ids[None, :]
    first_tile = jnp.sum(jnp.where(onehot, windows[0][None, :], 0), axis=1)
    after_tile = jnp.sum(jnp.where(onehot, windows[1][None, :], 0), axis=1)
    video_rows = cross_q.shape[0]
    video_tile = (position * video_rows + jnp.arange(video_rows, dtype=jnp.int32)) // TILE_LEN
    visible = (first_tile[None, :] <= video_tile[:, None]) & (
        video_tile[:, None] < after_tile[None, :]
    )
    state = absorb(
        start_state(video_rows, audio_heads, AUDIO_DIM),
        cross_q,
        near_keys,
        near_values,
        audio_heads,
        audio_scaling,
        visible,
    )
    video_cross = normalize_heads(state)
    return (video_self, audio_out, video_cross)


def solution(mesh):
    return jax.shard_map(
        body,
        mesh=mesh,
        in_specs=(
            P(("grp", "seq", "sub"), "head"),
            P(("grp", "seq", "sub"), "head"),
            P(("grp", "seq", "sub"), "head"),
            P(("grp", "seq", "sub"), "head"),
            P(("grp", "seq", "sub"), "head"),
            P(("grp", "seq", "sub"), "head"),
            P(("grp", "seq", "sub"), "head"),
            P(("grp", "seq", "sub"), "head"),
            P(("grp", "seq", "sub"), "head"),
            P(None, "grp"),
        ),
        out_specs=(
            P(("grp", "seq", "sub"), "head"),
            P(("grp", "seq", "sub"), "head"),
            P(("grp", "seq", "sub"), "head"),
        ),
        check_vma=False,
    )
```

profile of v0, /device:TPU:0, one launch (start us, length us, event | category | flops | bytes accessed | tf_op | source)
XLA Modules:
  0.0 218.2 jit_solution(4391640885050590359)
XLA Ops:
  8.4 5.1 %all_to_all.73 = bf16[160,2,1024]{2,0,1:T(8,128)(2,1)} all-to-all(bf16[160,2,1024]{2,0,1:T(8,128)(2,1)S(1)} %bitcast.132), channel_id=1, replica_groups=mesh['grp'=2,'seq'=4,'head'=2,'sub'=2] {'sub'}, dimensions={1} | all-to-all | bytes 1310720 | tf_op jit(solution)/shard_map/all_to_all | solution.py:100
  13.7 5.1 %all_to_all.74 = bf16[160,2,1024]{2,0,1:T(8,128)(2,1)} all-to-all(bf16[160,2,1024]{2,0,1:T(8,128)(2,1)S(1)} %bitcast.133), channel_id=1, replica_groups=mesh['grp'=2,'seq'=4,'head'=2,'sub'=2] {'sub'}, dimensions={1} | all-to-all | bytes 1310720 | tf_op jit(solution)/shard_map/all_to_all | solution.py:101
  20.9 3.7 %collective-permute-start = (bf16[40,2048]{1,0:T(8,128)(2,1)S(1)}, bf16[40,2048]{1,0:T(8,128)(2,1)}, u32[]{:S(2)}, u32[]{:S(2)}) collective-permute-start(bf16[40,2048]{1,0:T(8,128)(2,1)S(1)} %constant_dynamic-update-slice_fusion), channel_id=1, source_target_pairs={{0,1},{1,4},{4,5},{5,8},{8,9},{9,12},{12,13},{2,3},{3,6},{6,7},{7,... | collective-permute-start | bytes 491528 | tf_op jit(solution)/shard_map/ppermute | solution.py:22
  25.5 3.6 %all-to-all-start.1 = ((bf16[160,2,1024]{2,0,1:T(8,128)(2,1)}), bf16[160,2,1024]{2,0,1:T(8,128)(2,1)S(1)}, u32[]{:S(2)}, u32[]{:S(2)}) async-start(bf16[160,2,1024]{2,0,1:T(8,128)(2,1)} %bitcast.94), calls=%async_computation.1 | async-start | bytes 1310720 | tf_op jit(solution)/shard_map/all_to_all | solution.py:99
  35.9 36.1 %all-gather.5.cloned.1.call-done = bf16[1280,1024]{1,0:T(8,128)(2,1)} async-done(((bf16[320,1024]{1,0:T(8,128)(2,1)}), bf16[1280,1024]{1,0:T(8,128)(2,1)}) %all-gather.5.cloned.1.call-update) | async-done | bytes 2621456 | tf_op jit(solution)/shard_map/all_gather | solution.py:108
  72.0 55.8 %all-gather.7.cloned.1.call-done = bf16[1280,1024]{1,0:T(8,128)(2,1)} async-done(((bf16[320,1024]{1,0:T(8,128)(2,1)}), bf16[1280,1024]{1,0:T(8,128)(2,1)}) %all-gather.7.cloned.1.call-update) | async-done | bytes 2621456 | tf_op jit(solution)/shard_map/all_gather | solution.py:109
  127.8 35.4 %while.30 = (s32[]{:T(128)}, f32[8,320]{1,0:T(8,128)S(1)}, f32[8,320]{1,0:T(8,128)S(1)}, f32[8,320,128]{2,1,0:T(8,128)S(1)}, bf16[4,320,1024]{2,1,0:T(8,128)(2,1...) while((s32[]{:T(128)}, f32[8,320]{1,0:T(8,128)S(1)}, ...), condition=%wide.region_3.4_spmd.clone, body=%wide.region_0.3_spmd.clone.sunk | while | flops 426979840 | bytes 32931984 | solution.py:83
  129.3 2.5 %bitcast_reduce_fusion.2 = (f32[8,320]{1,0:T(8,128)S(1)}, f32[8,320,320]{2,1,0:T(8,128)}) fusion(bf16[320,8,128]{2,1,0:T(8,128)(2,1)S(1)} %bitcast.123, bf16[320,1024]{1,0:T(8,128)(2,1)S(1)} %get-tuple-element.365), kind=kOutput, calls=%fused_computation.1.clone.1 | convolution fusion | flops 211351040 | bytes 4597760 | tf_op jit(solution)/shard_map/while/body/eval_jaxpr/qhe,khe->hqk/dot_general | solution.py:44
  131.8 3.0 %fusion.59 = f32[8,320]{1,0:T(8,128)S(1)} fusion(f32[8,320,320]{2,1,0:T(8,128)} %get-tuple-element.325, f32[8,320]{1,0:T(8,128)S(1)} %select_maximum_fusion.4), kind=kLoop, calls=%fused_computation.4.clone.1 | loop fusion | flops 2455040 | bytes 3297280 | tf_op jit(solution)/shard_map/while/body/eval_jaxpr/reduce_sum | solution.py:57
  135.2 1.4 fusion.61
  138.1 2.5 %bitcast_reduce_fusion.2 = (f32[8,320]{1,0:T(8,128)S(1)}, f32[8,320,320]{2,1,0:T(8,128)}) fusion(bf16[320,8,128]{2,1,0:T(8,128)(2,1)S(1)} %bitcast.123, bf16[320,1024]{1,0:T(8,128)(2,1)S(1)} %get-tuple-element.365), kind=kOutput, calls=%fused_computation.1.clone.1 | convolution fusion | flops 211351040 | bytes 4597760 | tf_op jit(solution)/shard_map/while/body/eval_jaxpr/qhe,khe->hqk/dot_general | solution.py:44
  140.7 3.0 %fusion.59 = f32[8,320]{1,0:T(8,128)S(1)} fusion(f32[8,320,320]{2,1,0:T(8,128)} %get-tuple-element.325, f32[8,320]{1,0:T(8,128)S(1)} %select_maximum_fusion.4), kind=kLoop, calls=%fused_computation.4.clone.1 | loop fusion | flops 2455040 | bytes 3297280 | tf_op jit(solution)/shard_map/while/body/eval_jaxpr/reduce_sum | solution.py:57
  144.0 1.4 fusion.61
  145.5 1.4 dynamic-slice_bitcast_fusion.3
  147.0 2.5 %bitcast_reduce_fusion.2 = (f32[8,320]{1,0:T(8,128)S(1)}, f32[8,320,320]{2,1,0:T(8,128)}) fusion(bf16[320,8,128]{2,1,0:T(8,128)(2,1)S(1)} %bitcast.123, bf16[320,1024]{1,0:T(8,128)(2,1)S(1)} %get-tuple-element.365), kind=kOutput, calls=%fused_computation.1.clone.1 | convolution fusion | flops 211351040 | bytes 4597760 | tf_op jit(solution)/shard_map/while/body/eval_jaxpr/qhe,khe->hqk/dot_general | solution.py:44
  149.5 3.0 %fusion.59 = f32[8,320]{1,0:T(8,128)S(1)} fusion(f32[8,320,320]{2,1,0:T(8,128)} %get-tuple-element.325, f32[8,320]{1,0:T(8,128)S(1)} %select_maximum_fusion.4), kind=kLoop, calls=%fused_computation.4.clone.1 | loop fusion | flops 2455040 | bytes 3297280 | tf_op jit(solution)/shard_map/while/body/eval_jaxpr/reduce_sum | solution.py:57
  152.9 1.4 fusion.61
  154.3 1.4 dynamic-slice_bitcast_fusion.3
  155.9 2.5 %bitcast_reduce_fusion.2 = (f32[8,320]{1,0:T(8,128)S(1)}, f32[8,320,320]{2,1,0:T(8,128)}) fusion(bf16[320,8,128]{2,1,0:T(8,128)(2,1)S(1)} %bitcast.123, bf16[320,1024]{1,0:T(8,128)(2,1)S(1)} %get-tuple-element.365), kind=kOutput, calls=%fused_computation.1.clone.1 | convolution fusion | flops 211351040 | bytes 4597760 | tf_op jit(solution)/shard_map/while/body/eval_jaxpr/qhe,khe->hqk/dot_general | solution.py:44
  158.4 3.0 %fusion.59 = f32[8,320]{1,0:T(8,128)S(1)} fusion(f32[8,320,320]{2,1,0:T(8,128)} %get-tuple-element.325, f32[8,320]{1,0:T(8,128)S(1)} %select_maximum_fusion.4), kind=kLoop, calls=%fused_computation.4.clone.1 | loop fusion | flops 2455040 | bytes 3297280 | tf_op jit(solution)/shard_map/while/body/eval_jaxpr/reduce_sum | solution.py:57
  161.7 1.4 fusion.61
  164.3 4.4 %all_to_all.75 = bf16[2,160,1024]{2,1,0:T(8,128)(2,1)S(1)} all-to-all(bf16[2,160,1024]{2,1,0:T(8,128)(2,1)S(1)} %convert_element_type.36), channel_id=1, replica_groups=mesh['grp'=2,'seq'=4,'head'=2,'sub'=2] {'sub'}, dimensions={0} | all-to-all | bytes 1310720 | tf_op jit(solution)/shard_map/all_to_all | solution.py:113
  169.6 26.7 %all-gather.11.cloned.1.call-done = bf16[1280,1024]{1,0:T(8,128)(2,1)} async-done(((bf16[160,1024]{1,0:T(8,128)(2,1)}), bf16[1280,1024]{1,0:T(8,128)(2,1)}) %all-gather.11.cloned.1.call-update) | async-done | bytes 2621456 | tf_op jit(solution)/shard_map/all_gather | solution.py:121
  196.3 14.4 %while.31 = (s32[]{:T(128)}, f32[16,40]{1,0:T(8,128)S(1)}, f32[16,40]{1,0:T(8,128)S(1)}, f32[16,40,64]{2,1,0:T(8,128)S(1)}, bf16[4,320,1024]{2,1,0:T(8,128)(2,1)...) while((s32[]{:T(128)}, f32[16,40]{1,0:T(8,128)S(1)}, ...), condition=%wide.region_7.8_spmd.clone, body=%wide.region_4.7_spmd.clone.sunk | while | flops 53783680 | bytes 9625717 | solution.py:83
  (133 shorter events, 32.5 us)
Async XLA Ops:
  7.2 64.8 %all-gather.5.cloned.1.call-start = ((), (), s32[]{:S(2)}) async-start(), calls=%async_computation.4 | async-start | bytes 3276800 | tf_op jit(solution)/shard_map/all_gather | solution.py:108
  8.3 5.2 %copy-start.2 = (bf16[160,2048]{1,0:T(8,128)(2,1)S(1)}, bf16[160,2048]{1,0:T(8,128)(2,1)}, u32[]{:S(2)}) copy-start(bf16[160,2048]{1,0:T(8,128)(2,1)} %param.16) | copy-start | bytes 1966084
  13.5 114.2 %all-gather.7.cloned.1.call-start = ((), (), s32[]{:S(2)}) async-start(), calls=%async_computation.5 | async-start | bytes 3276800 | tf_op jit(solution)/shard_map/all_gather | solution.py:109
  13.6 5.9 %copy-start.6 = (bf16[40,1024]{1,0:T(8,128)(2,1)S(1)}, bf16[40,1024]{1,0:T(8,128)(2,1)}, u32[]{:S(2)}) copy-start(bf16[40,1024]{1,0:T(8,128)(2,1)} %param.21) | copy-start | bytes 245764
  13.7 6.0 %copy-start.7 = (bf16[40,1024]{1,0:T(8,128)(2,1)S(1)}, bf16[40,1024]{1,0:T(8,128)(2,1)}, u32[]{:S(2)}) copy-start(bf16[40,1024]{1,0:T(8,128)(2,1)} %param.22) | copy-start | bytes 245764
  13.7 11.0 %copy-start.3 = (bf16[160,2048]{1,0:T(8,128)(2,1)S(1)}, bf16[160,2048]{1,0:T(8,128)(2,1)}, u32[]{:S(2)}) copy-start(bf16[160,2048]{1,0:T(8,128)(2,1)} %param.14) | copy-start | bytes 1966084
  18.8 150.8 %all-gather.9.cloned.1.call-start = ((), (), s32[]{:S(2)}) async-start(), calls=%async_computation.6 | async-start | bytes 2949120 | tf_op jit(solution)/shard_map/all_gather | solution.py:120
  19.6 10.7 %collective-permute-start.1 = (bf16[40,2048]{1,0:T(8,128)(2,1)S(1)}, bf16[40,2048]{1,0:T(8,128)(2,1)}, u32[]{:S(2)}, u32[]{:S(2)}) collective-permute-start(bf16[40,2048]{1,0:T(8,128)(2,1)S(1)} %constant_dynamic-update-slice_fusion), channel_id=1, source_target_pairs={{1,0},{4,1},{5,4},{8,5},{9,8},{12,9},{13,12},{3,2},{6,3},{7,6},{10... | collective-permute-start | bytes 491528 | tf_op jit(solution)/shard_map/ppermute | solution.py:24
  20.9 9.4 %collective-permute-start = (bf16[40,2048]{1,0:T(8,128)(2,1)S(1)}, bf16[40,2048]{1,0:T(8,128)(2,1)}, u32[]{:S(2)}, u32[]{:S(2)}) collective-permute-start(bf16[40,2048]{1,0:T(8,128)(2,1)S(1)} %constant_dynamic-update-slice_fusion), channel_id=1, source_target_pairs={{0,1},{1,4},{4,5},{5,8},{8,9},{9,12},{12,13},{2,3},{3,6},{6,7},{7,... | collective-permute-start | bytes 491528 | tf_op jit(solution)/shard_map/ppermute | solution.py:22
  24.6 5.2 %copy-start.4 = (bf16[160,1024]{1,0:T(8,128)(2,1)S(1)}, bf16[160,1024]{1,0:T(8,128)(2,1)}, u32[]{:S(2)}) copy-start(bf16[160,1024]{1,0:T(8,128)(2,1)} %param.20) | copy-start | bytes 983044
  25.5 4.5 %copy-start.8 = (s32[2,40]{1,0:T(2,128)S(1)}, s32[2,40]{1,0:T(2,128)}, u32[]{:S(2)}) copy-start(s32[2,40]{1,0:T(2,128)} %param.23) | copy-start | bytes 964
  25.5 10.4 %all-to-all-start.1 = ((bf16[160,2,1024]{2,0,1:T(8,128)(2,1)}), bf16[160,2,1024]{2,0,1:T(8,128)(2,1)S(1)}, u32[]{:S(2)}, u32[]{:S(2)}) async-start(bf16[160,2,1024]{2,0,1:T(8,128)(2,1)} %bitcast.94), calls=%async_computation.1 | async-start | bytes 1310720 | tf_op jit(solution)/shard_map/all_to_all | solution.py:99
  29.2 167.1 %all-gather.11.cloned.1.call-start = ((), (), s32[]{:S(2)}) async-start(), calls=%async_computation.7 | async-start | bytes 2949120 | tf_op jit(solution)/shard_map/all_gather | solution.py:121
  32.4 1.9 copy-start.5
  131.8 3.4 %copy-start = (f32[8,320,320]{2,1,0:T(8,128)S(1)}, f32[8,320,320]{2,1,0:T(8,128)}, u32[]{:S(2)}) copy-start(f32[8,320,320]{2,1,0:T(8,128)} %get-tuple-element.325) | copy-start | bytes 9830404 | tf_op jit(solution)/shard_map/while
  140.7 3.4 %copy-start = (f32[8,320,320]{2,1,0:T(8,128)S(1)}, f32[8,320,320]{2,1,0:T(8,128)}, u32[]{:S(2)}) copy-start(f32[8,320,320]{2,1,0:T(8,128)} %get-tuple-element.325) | copy-start | bytes 9830404 | tf_op jit(solution)/shard_map/while
  149.5 3.4 %copy-start = (f32[8,320,320]{2,1,0:T(8,128)S(1)}, f32[8,320,320]{2,1,0:T(8,128)}, u32[]{:S(2)}) copy-start(f32[8,320,320]{2,1,0:T(8,128)} %get-tuple-element.325) | copy-start | bytes 9830404 | tf_op jit(solution)/shard_map/while
  158.4 3.3 %copy-start = (f32[8,320,320]{2,1,0:T(8,128)S(1)}, f32[8,320,320]{2,1,0:T(8,128)}, u32[]{:S(2)}) copy-start(f32[8,320,320]{2,1,0:T(8,128)} %get-tuple-element.325) | copy-start | bytes 9830404 | tf_op jit(solution)/shard_map/while
  164.3 32.0 %copy-start.1 = (bf16[40,1024]{1,0:T(8,128)(2,1)S(1)}, bf16[40,1024]{1,0:T(8,128)(2,1)}, u32[]{:S(2)}) copy-start(bf16[40,1024]{1,0:T(8,128)(2,1)} %param.17) | copy-start | bytes 245764
Sparse Core Ops, SparseCore 0:
  13.6 58.2 all-gather.4
  73.6 54.1 all-gather.6
  129.4 32.4 all-gather.8
  163.4 32.8 all-gather.10
where the time goes:
time: 219 us; the launch traced here: 218 us
  waiting for transfers between devices  120 us (55%)
  local copies, waits for them, and re-layouts  23.1 us (11%)
  matrix products  20.8 us (9%)
  other arithmetic  16.4 us (7%)
  blocking collectives  14.7 us (7%)
  between operations  14.1 us (6%)
  starting transfers between devices  8.81 us (4%)
    all_gather x1, waiting for transfers between devices, body(): lax.all_gather(moved_v, 'seq', axis=0, tiled=True)  55.8 us
    all_gather x1, waiting for transfers between devices, body(): lax.all_gather(moved_k, 'seq', axis=0, tiled=True)  36.1 us
    all_gather x1, waiting for transfers between devices, body(): lax.all_gather(cross_v, ('seq', 'sub'), axis=0, tiled=True)  26.7 us
    reduce_sum x9, other arithmetic, absorb(): summed = summed * shrink + jnp.sum(weights, axis=2)  14.4 us
    dot_general x9, matrix products, absorb(): jnp.einsum('qhe,khe->hqk', queries.reshape(query_count, head_count, head_...  12.6 us
    dynamic_slice x12, local copies, waits for them, and re-layouts, fold_keys(): result, unused = lax.scan(one_block, state_in, (key_blocks, value_blocks))  8.35 us
    dot_general x9, matrix products, absorb(): jnp.einsum('hqk,khe->hqe', weights.astype(jnp.bfloat16), value_rows.resha...  8.23 us
    while x28, local copies, waits for them, and re-layouts  7.43 us
  transfers between devices with their start and end apart: 7, of which 3 were waited for; matrix products, arithmetic and copies ran while one was open for 20% of the time, Pallas kernels for 0%

commit v1 on v0

--- a/solution.py
+++ b/solution.py
@@ -4,6 +4,7 @@
 import jax.numpy as jnp
 from jax import lax
 from jax.sharding import PartitionSpec as P
+from jax.lax import all_to_all, axis_size
 
 HEAD_DIM = 128
 AUDIO_DIM = 64
@@ -102,12 +103,12 @@
     )
     pair_heads = video_heads // lax.axis_size("sub")
     folder = partial(fold_keys, queries=moved_q, head_count=pair_heads, scaling=video_scaling)
+    supply_all_sites = lambda s0: jnp.concatenate(
+        all_to_all(jnp.stack([s0] * axis_size("seq"), 0), "seq", 0, 0), 0
+    )
     state = folder(
         start_state(moved_q.shape[0], pair_heads, HEAD_DIM),
-        (
-            lax.all_gather(moved_k, "seq", axis=0, tiled=True),
-            lax.all_gather(moved_v, "seq", axis=0, tiled=True),
-        ),
+        (supply_all_sites(moved_k), lax.all_gather(moved_v, "seq", axis=0, tiled=True)),
         jnp.int32(0),
     )
     video_self = lax.all_to_all(

time: 219 us -> 208 us (0.950)
  waiting for transfers between devices: 120 us -> 101 us
  starting transfers between devices: 8.81 us -> 15.1 us
    all_to_all x1 -> x2, waiting for transfers between devices: 0.01 us -> 84.2 us  [the longest x1 82.4 us: body(): all_to_all(jnp.stack([s0] * axis_size('seq'), 0), 'seq', 0, 0)]
    all_gather x1, waiting for transfers between devices: 55.8 us -> 0.01 us  [body(): lax.all_gather(moved_v, 'seq', axis=0, tiled=True)]
    all_gather x1 -> x0, waiting for transfers between devices: 36.1 us -> none  [body(): lax.all_gather(moved_k, 'seq', axis=0, tiled=True)]
    all_gather x1, waiting for transfers between devices: 26.7 us -> 16.1 us  [body(): lax.all_gather(cross_v, ('seq', 'sub'), axis=0, tiled=True)]
    all_to_all x1 -> x2, starting transfers between devices: 3.64 us -> 9.99 us  [the longest x1 6.48 us: body(): all_to_all(jnp.stack([s0] * axis_size('seq'), 0), 'seq', 0, 0)]
  transfers between devices with their start and end apart: 7 -> 7, of which waited for: 3 -> 3; matrix products, arithmetic and copies ran while one was open for 20% -> 22% of each run, Pallas kernels for 0% -> 0%
where the time goes in v1:
time: 208 us; the launch traced here: 207 us
  waiting for transfers between devices  101 us (49%)
  local copies, waits for them, and re-layouts  25 us (12%)
  matrix products  20.8 us (10%)
  other arithmetic  16.6 us (8%)
  starting transfers between devices  15.1 us (7%)
  between operations  14.1 us (7%)
  blocking collectives  13.9 us (7%)
    all_to_all x1, waiting for transfers between devices, body(): all_to_all(jnp.stack([s0] * axis_size('seq'), 0), 'seq', 0, 0)  82.4 us
    all_gather x1, waiting for transfers between devices, body(): lax.all_gather(cross_v, ('seq', 'sub'), axis=0, tiled=True)  16.1 us
    reduce_sum x9, other arithmetic, absorb(): summed = summed * shrink + jnp.sum(weights, axis=2)  14.6 us
    dot_general x9, matrix products, absorb(): jnp.einsum('qhe,khe->hqk', queries.reshape(query_count, head_count, head_...  12.6 us
    dynamic_slice x12, local copies, waits for them, and re-layouts, fold_keys(): result, unused = lax.scan(one_block, state_in, (key_blocks, value_blocks))  8.35 us
    dot_general x9, matrix products, absorb(): jnp.einsum('hqk,khe->hqe', weights.astype(jnp.bfloat16), value_rows.resha...  8.23 us
    while x28, local copies, waits for them, and re-layouts  7.42 us
    all_to_all x1, starting transfers between devices, body(): all_to_all(jnp.stack([s0] * axis_size('seq'), 0), 'seq', 0, 0)  6.48 us
  transfers between devices with their start and end apart: 7, of which 3 were waited for; matrix products, arithmetic and copies ran while one was open for 22% of the time, Pallas kernels for 0%

profile of v1, /device:TPU:0, one launch (start us, length us, event | category | flops | bytes accessed | tf_op | source)
XLA Modules:
  0.0 207.0 jit_solution(1417688503916554767)
XLA Ops:
  8.4 5.2 %all_to_all.75 = bf16[160,2,1024]{2,0,1:T(8,128)(2,1)} all-to-all(bf16[160,2,1024]{2,0,1:T(8,128)(2,1)S(1)} %bitcast.130), channel_id=1, replica_groups=mesh['grp'=2,'seq'=4,'head'=2,'sub'=2] {'sub'}, dimensions={1} | all-to-all | bytes 1310720 | tf_op jit(solution)/shard_map/all_to_all | solution.py:102
  15.2 3.5 %all-to-all-start = ((bf16[160,2,1024]{2,0,1:T(8,128)(2,1)}), bf16[160,2,1024]{2,0,1:T(8,128)(2,1)S(1)}, u32[]{:S(2)}, u32[]{:S(2)}) async-start(bf16[160,2,1024]{2,0,1:T(8,128)(2,1)} %bitcast.94), calls=%async_computation | async-start | bytes 1310720 | tf_op jit(solution)/shard_map/all_to_all | solution.py:101
  18.8 1.8 all-to-all-done
  20.6 4.2 %all_to_all.76 = bf16[160,2,1024]{2,0,1:T(8,128)(2,1)S(1)} all-to-all(bf16[160,2,1024]{2,0,1:T(8,128)(2,1)S(1)} %bitcast.128), channel_id=1, replica_groups=mesh['grp'=2,'seq'=4,'head'=2,'sub'=2] {'sub'}, dimensions={1} | all-to-all | bytes 1310720 | tf_op jit(solution)/shard_map/all_to_all | solution.py:100
  24.8 1.9 stack.10
  26.7 6.5 %all-to-all-start.1 = ((bf16[4,320,1024]{2,1,0:T(8,128)(2,1)}), bf16[4,320,1024]{2,1,0:T(8,128)(2,1)}, u32[]{:S(2)}, u32[]{:S(2)}) async-start(bf16[4,320,1024]{2,1,0:T(8,128)(2,1)} %stack.10), calls=%async_computation.1 | async-start | bytes 5242880 | tf_op jit(solution)/shard_map/all_to_all | solution.py:107
  34.5 3.7 %collective-permute-start = (bf16[40,2048]{1,0:T(8,128)(2,1)S(1)}, bf16[40,2048]{1,0:T(8,128)(2,1)}, u32[]{:S(2)}, u32[]{:S(2)}) collective-permute-start(bf16[40,2048]{1,0:T(8,128)(2,1)S(1)} %constant_dynamic-update-slice_fusion), channel_id=1, source_target_pairs={{0,1},{1,4},{4,5},{5,8},{8,9},{9,12},{12,13},{2,3},{3,6},{6,7},{7,... | collective-permute-start | bytes 491528 | tf_op jit(solution)/shard_map/ppermute | solution.py:23
  44.4 82.4 %all-to-all-done.1 = bf16[4,320,1024]{2,1,0:T(8,128)(2,1)} async-done(((bf16[4,320,1024]{2,1,0:T(8,128)(2,1)}), bf16[4,320,1024]{2,1,0:T(8,128)(2,1)}, u32[]{:S(2)}, u32[]{:S(2)}) %all-to-all-start.1) | async-done | bytes 2621472 | tf_op jit(solution)/shard_map/all_to_all | solution.py:107
  126.8 35.6 %while.30 = (s32[]{:T(128)}, f32[8,320]{1,0:T(8,128)S(1)}, f32[8,320]{1,0:T(8,128)S(1)}, f32[8,320,128]{2,1,0:T(8,128)S(1)}, bf16[4,320,1024]{2,1,0:T(8,128)(2,1...) while((s32[]{:T(128)}, f32[8,320]{1,0:T(8,128)S(1)}, ...), condition=%wide.region_3.4_spmd.clone, body=%wide.region_0.3_spmd.clone.sunk | while | flops 426979840 | bytes 32931984 | solution.py:84
  128.3 2.5 %bitcast_reduce_fusion.2 = (f32[8,320]{1,0:T(8,128)S(1)}, f32[8,320,320]{2,1,0:T(8,128)}) fusion(bf16[320,8,128]{2,1,0:T(8,128)(2,1)S(1)} %bitcast.122, bf16[320,1024]{1,0:T(8,128)(2,1)S(1)} %get-tuple-element.365), kind=kOutput, calls=%fused_computation.1.clone.1 | convolution fusion | flops 211351040 | bytes 4597760 | tf_op jit(solution)/shard_map/while/body/eval_jaxpr/qhe,khe->hqk/dot_general | solution.py:45
  130.9 3.0 %fusion.59 = f32[8,320]{1,0:T(8,128)S(1)} fusion(f32[8,320,320]{2,1,0:T(8,128)} %get-tuple-element.325, f32[8,320]{1,0:T(8,128)S(1)} %select_maximum_fusion.4), kind=kLoop, calls=%fused_computation.4.clone.1 | loop fusion | flops 2455040 | bytes 3297280 | tf_op jit(solution)/shard_map/while/body/eval_jaxpr/reduce_sum | solution.py:58
  134.2 1.4 fusion.61
  137.1 2.5 %bitcast_reduce_fusion.2 = (f32[8,320]{1,0:T(8,128)S(1)}, f32[8,320,320]{2,1,0:T(8,128)}) fusion(bf16[320,8,128]{2,1,0:T(8,128)(2,1)S(1)} %bitcast.122, bf16[320,1024]{1,0:T(8,128)(2,1)S(1)} %get-tuple-element.365), kind=kOutput, calls=%fused_computation.1.clone.1 | convolution fusion | flops 211351040 | bytes 4597760 | tf_op jit(solution)/shard_map/while/body/eval_jaxpr/qhe,khe->hqk/dot_general | solution.py:45
  139.6 3.0 %fusion.59 = f32[8,320]{1,0:T(8,128)S(1)} fusion(f32[8,320,320]{2,1,0:T(8,128)} %get-tuple-element.325, f32[8,320]{1,0:T(8,128)S(1)} %select_maximum_fusion.4), kind=kLoop, calls=%fused_computation.4.clone.1 | loop fusion | flops 2455040 | bytes 3297280 | tf_op jit(solution)/shard_map/while/body/eval_jaxpr/reduce_sum | solution.py:58
  143.0 1.4 fusion.61
  145.9 2.5 %bitcast_reduce_fusion.2 = (f32[8,320]{1,0:T(8,128)S(1)}, f32[8,320,320]{2,1,0:T(8,128)}) fusion(bf16[320,8,128]{2,1,0:T(8,128)(2,1)S(1)} %bitcast.122, bf16[320,1024]{1,0:T(8,128)(2,1)S(1)} %get-tuple-element.365), kind=kOutput, calls=%fused_computation.1.clone.1 | convolution fusion | flops 211351040 | bytes 4597760 | tf_op jit(solution)/shard_map/while/body/eval_jaxpr/qhe,khe->hqk/dot_general | solution.py:45
  148.5 3.0 %fusion.59 = f32[8,320]{1,0:T(8,128)S(1)} fusion(f32[8,320,320]{2,1,0:T(8,128)} %get-tuple-element.325, f32[8,320]{1,0:T(8,128)S(1)} %select_maximum_fusion.4), kind=kLoop, calls=%fused_computation.4.clone.1 | loop fusion | flops 2455040 | bytes 3297280 | tf_op jit(solution)/shard_map/while/body/eval_jaxpr/reduce_sum | solution.py:58
  151.8 1.4 fusion.61
  154.7 2.5 %bitcast_reduce_fusion.2 = (f32[8,320]{1,0:T(8,128)S(1)}, f32[8,320,320]{2,1,0:T(8,128)}) fusion(bf16[320,8,128]{2,1,0:T(8,128)(2,1)S(1)} %bitcast.122, bf16[320,1024]{1,0:T(8,128)(2,1)S(1)} %get-tuple-element.365), kind=kOutput, calls=%fused_computation.1.clone.1 | convolution fusion | flops 211351040 | bytes 4597760 | tf_op jit(solution)/shard_map/while/body/eval_jaxpr/qhe,khe->hqk/dot_general | solution.py:45
  157.3 3.1 %fusion.59 = f32[8,320]{1,0:T(8,128)S(1)} fusion(f32[8,320,320]{2,1,0:T(8,128)} %get-tuple-element.325, f32[8,320]{1,0:T(8,128)S(1)} %select_maximum_fusion.4), kind=kLoop, calls=%fused_computation.4.clone.1 | loop fusion | flops 2455040 | bytes 3297280 | tf_op jit(solution)/shard_map/while/body/eval_jaxpr/reduce_sum | solution.py:58
  161.0 1.4 fusion.61
  163.5 4.5 %all_to_all.77 = bf16[2,160,1024]{2,1,0:T(8,128)(2,1)S(1)} all-to-all(bf16[2,160,1024]{2,1,0:T(8,128)(2,1)S(1)} %convert_element_type.36), channel_id=1, replica_groups=mesh['grp'=2,'seq'=4,'head'=2,'sub'=2] {'sub'}, dimensions={0} | all-to-all | bytes 1310720 | tf_op jit(solution)/shard_map/all_to_all | solution.py:114
  168.9 16.1 %all-gather.8.cloned.1.call-done = bf16[1280,1024]{1,0:T(8,128)(2,1)} async-done(((bf16[160,1024]{1,0:T(8,128)(2,1)}), bf16[1280,1024]{1,0:T(8,128)(2,1)}) %all-gather.8.cloned.1.call-update) | async-done | bytes 2621456 | tf_op jit(solution)/shard_map/all_gather | solution.py:122
  185.0 14.4 %while.31 = (s32[]{:T(128)}, f32[16,40]{1,0:T(8,128)S(1)}, f32[16,40]{1,0:T(8,128)S(1)}, f32[16,40,64]{2,1,0:T(8,128)S(1)}, bf16[4,320,1024]{2,1,0:T(8,128)(2,1)...) while((s32[]{:T(128)}, f32[16,40]{1,0:T(8,128)S(1)}, ...), condition=%wide.region_7.8_spmd.clone, body=%wide.region_4.7_spmd.clone.sunk | while | flops 53783680 | bytes 9625717 | solution.py:84
  (133 shorter events, 34.8 us)
Async XLA Ops:
  7.2 119.6 %all-gather.4.cloned.1.call-start = ((), (), s32[]{:S(2)}) async-start(), calls=%async_computation.5 | async-start | bytes 3276800 | tf_op jit(solution)/shard_map/all_gather | solution.py:111
  8.3 6.0 %copy-start.2 = (bf16[160,2048]{1,0:T(8,128)(2,1)S(1)}, bf16[160,2048]{1,0:T(8,128)(2,1)}, u32[]{:S(2)}) copy-start(bf16[160,2048]{1,0:T(8,128)(2,1)} %param.15) | copy-start | bytes 1966084
  13.6 155.3 %all-gather.6.cloned.1.call-start = ((), (), s32[]{:S(2)}) async-start(), calls=%async_computation.6 | async-start | bytes 2949120 | tf_op jit(solution)/shard_map/all_gather | solution.py:121
  14.3 4.4 %copy-start.3 = (bf16[160,2048]{1,0:T(8,128)(2,1)S(1)}, bf16[160,2048]{1,0:T(8,128)(2,1)}, u32[]{:S(2)}) copy-start(bf16[160,2048]{1,0:T(8,128)(2,1)} %param.14) | copy-start | bytes 1966084
  15.2 5.3 %all-to-all-start = ((bf16[160,2,1024]{2,0,1:T(8,128)(2,1)}), bf16[160,2,1024]{2,0,1:T(8,128)(2,1)S(1)}, u32[]{:S(2)}, u32[]{:S(2)}) async-start(bf16[160,2,1024]{2,0,1:T(8,128)(2,1)} %bitcast.94), calls=%async_computation | async-start | bytes 1310720 | tf_op jit(solution)/shard_map/all_to_all | solution.py:101
  26.7 6.5 %copy-start.6 = (bf16[40,1024]{1,0:T(8,128)(2,1)S(1)}, bf16[40,1024]{1,0:T(8,128)(2,1)}, u32[]{:S(2)}) copy-start(bf16[40,1024]{1,0:T(8,128)(2,1)} %param.21) | copy-start | bytes 245764
  26.7 6.5 %copy-start.7 = (bf16[40,1024]{1,0:T(8,128)(2,1)S(1)}, bf16[40,1024]{1,0:T(8,128)(2,1)}, u32[]{:S(2)}) copy-start(bf16[40,1024]{1,0:T(8,128)(2,1)} %param.22) | copy-start | bytes 245764
  26.7 11.6 %copy-start.4 = (bf16[160,1024]{1,0:T(8,128)(2,1)S(1)}, bf16[160,1024]{1,0:T(8,128)(2,1)}, u32[]{:S(2)}) copy-start(bf16[160,1024]{1,0:T(8,128)(2,1)} %param.20) | copy-start | bytes 983044
  26.7 100.1 %all-to-all-start.1 = ((bf16[4,320,1024]{2,1,0:T(8,128)(2,1)}), bf16[4,320,1024]{2,1,0:T(8,128)(2,1)}, u32[]{:S(2)}, u32[]{:S(2)}) async-start(bf16[4,320,1024]{2,1,0:T(8,128)(2,1)} %stack.10), calls=%async_computation.1 | async-start | bytes 5242880 | tf_op jit(solution)/shard_map/all_to_all | solution.py:107
  33.1 5.4 %copy-start.8 = (s32[2,40]{1,0:T(2,128)S(1)}, s32[2,40]{1,0:T(2,128)}, u32[]{:S(2)}) copy-start(s32[2,40]{1,0:T(2,128)} %param.23) | copy-start | bytes 964
  33.1 151.8 %all-gather.8.cloned.1.call-start = ((), (), s32[]{:S(2)}) async-start(), calls=%async_computation.7 | async-start | bytes 2949120 | tf_op jit(solution)/shard_map/all_gather | solution.py:122
  33.2 5.6 %collective-permute-start.1 = (bf16[40,2048]{1,0:T(8,128)(2,1)S(1)}, bf16[40,2048]{1,0:T(8,128)(2,1)}, u32[]{:S(2)}, u32[]{:S(2)}) collective-permute-start(bf16[40,2048]{1,0:T(8,128)(2,1)S(1)} %constant_dynamic-update-slice_fusion), channel_id=1, source_target_pairs={{1,0},{4,1},{5,4},{8,5},{9,8},{12,9},{13,12},{3,2},{6,3},{7,6},{10... | collective-permute-start | bytes 491528 | tf_op jit(solution)/shard_map/ppermute | solution.py:25
  34.5 4.3 %collective-permute-start = (bf16[40,2048]{1,0:T(8,128)(2,1)S(1)}, bf16[40,2048]{1,0:T(8,128)(2,1)}, u32[]{:S(2)}, u32[]{:S(2)}) collective-permute-start(bf16[40,2048]{1,0:T(8,128)(2,1)S(1)} %constant_dynamic-update-slice_fusion), channel_id=1, source_target_pairs={{0,1},{1,4},{4,5},{5,8},{8,9},{9,12},{12,13},{2,3},{3,6},{6,7},{7,... | collective-permute-start | bytes 491528 | tf_op jit(solution)/shard_map/ppermute | solution.py:23
  40.9 1.9 copy-start.5
  130.9 3.3 %copy-start = (f32[8,320,320]{2,1,0:T(8,128)S(1)}, f32[8,320,320]{2,1,0:T(8,128)}, u32[]{:S(2)}) copy-start(f32[8,320,320]{2,1,0:T(8,128)} %get-tuple-element.325) | copy-start | bytes 9830404 | tf_op jit(solution)/shard_map/while
  139.6 3.4 %copy-start = (f32[8,320,320]{2,1,0:T(8,128)S(1)}, f32[8,320,320]{2,1,0:T(8,128)}, u32[]{:S(2)}) copy-start(f32[8,320,320]{2,1,0:T(8,128)} %get-tuple-element.325) | copy-start | bytes 9830404 | tf_op jit(solution)/shard_map/while
  148.5 3.3 %copy-start = (f32[8,320,320]{2,1,0:T(8,128)S(1)}, f32[8,320,320]{2,1,0:T(8,128)}, u32[]{:S(2)}) copy-start(f32[8,320,320]{2,1,0:T(8,128)} %get-tuple-element.325) | copy-start | bytes 9830404 | tf_op jit(solution)/shard_map/while
  157.3 3.7 %copy-start = (f32[8,320,320]{2,1,0:T(8,128)S(1)}, f32[8,320,320]{2,1,0:T(8,128)}, u32[]{:S(2)}) copy-start(f32[8,320,320]{2,1,0:T(8,128)} %get-tuple-element.325) | copy-start | bytes 9830404 | tf_op jit(solution)/shard_map/while
  163.5 21.5 %copy-start.1 = (bf16[40,1024]{1,0:T(8,128)(2,1)S(1)}, bf16[40,1024]{1,0:T(8,128)(2,1)}, u32[]{:S(2)}) copy-start(bf16[40,1024]{1,0:T(8,128)(2,1)} %param.17) | copy-start | bytes 245764
Sparse Core Ops, SparseCore 0:
  13.7 102.3 all-gather.3
  117.7 33.2 all-gather.5
  152.7 32.2 all-gather.7
